TPU v7x, 32 devices: a whole 2x2x4 slice. The times are simulated.
32 devices in a mesh: group: 4 (over z), row: 2 (over x), col: 4 (over y, core).
Axes of the slice: x: 2, y: 2, z: 4, core: 2. Of those that a mesh axis runs over, the one named last changes fastest.
Arguments:
- child_front: float32 [4, 4, 4, 128, 8, 2, 128], P('group', None, 'col', None, None, 'row'), as said below
- top_front: float32 [12, 4, 4, 32, 24, 2, 128], P(None, 'col', 'group', None, None, 'row'), as said below
- block_map: int32 [4, 8], replicated, may hold values from 0 to 47, as said below
- pivots: int32 [4], P('group'), may hold values from 512 to 1024, as said below
- noise: float32 [4, 1024], P('group'), may hold values from -6 to 6
- top_sample: float32 [6144], replicated, may hold values from -12 to 12
Outputs:
- top_out: float32 [12, 4, 4, 32, 24, 2, 128], P(None, 'col', 'group', None, None, 'row')
- child_sample: float32 [4, 1024], P('group')
Inputs may be any that keep to these rules, and one draw needn't show every extreme that they name: `child_front`: each child front is symmetric positive definite. `top_front`: symmetric positive definite. block_map[g, u] mod 8 equals u; the entries of one row are distinct. `pivots`: A multiple of 128; some child has 1024.
All inputs are finite; a program needn't handle non-finite values.
Results may differ from a plain program's by a relative error of at most 0.00015.
Values sent between devices are 32-bit elements; how exact they have to be, the bound alone decides.
A program may use at most 64 MiB of HBM per device.

v0:
```python
import functools
import math

import jax
import jax.numpy as jnp
from jax import lax
from jax.experimental import pallas as pl
from jax.experimental.pallas import tpu as pltpu
from jax.sharding import PartitionSpec as P

MESH = pl.DeviceIdType.MESH
HIGH = lax.Precision.HIGHEST
SUB = 8
VMEM = pl.BlockSpec(memory_space=pltpu.VMEM)
SMEM = pl.BlockSpec(memory_space=pltpu.SMEM)


def split(x):
    high = x.astype(jnp.bfloat16)
    low = (x - high.astype(jnp.float32)).astype(jnp.bfloat16)
    return high, low


def dot3(left, right, dims):
    lh, ll = left
    rh, rl = right
    d = functools.partial(
        lax.dot_general, dimension_numbers=(dims, ((), ())), preferred_element_type=jnp.float32
    )
    return d(lh, rh) + (d(lh, rl) + d(ll, rh))


NN = ((1,), (0,))
TN = ((0,), (0,))
NT = ((1,), (1,))


def unit_inverse(rows_in):
    count = len(rows_in)
    width = rows_in[0].shape[1]
    strips = list(rows_in)
    lane = lax.broadcasted_iota(jnp.int32, (SUB, width), 1)
    sub = lax.broadcasted_iota(jnp.int32, (SUB, width), 0)
    result = []

    def row_of(x, i):
        return jnp.broadcast_to(x[i : i + 1, :], (SUB, width))

    for p in range(count):
        base = p * SUB
        strip = strips[p]
        cols = [
            jnp.broadcast_to(strip[:, base + j : base + j + 1], (SUB, width)) for j in range(SUB)
        ]
        scale, taps, rows = [], {}, []
        pivots = jnp.zeros((SUB, width), jnp.float32)
        for i in range(SUB):
            pivot = row_of(cols[i], i)
            recip = 1.0 / pivot
            scale.append(recip)
            pivots = jnp.where(sub == i, pivot, pivots)
            if i + 1 < SUB:
                factor = jnp.where(sub > i, cols[i] * recip, 0.0)
                for j in range(i + 1, SUB):
                    tap = row_of(cols[j], i)
                    taps[i, j] = tap
                    cols[j] = cols[j] - factor * tap
            at = lane == base + i
            row = jnp.where(at, 1.0, row_of(strip, i))
            rows.append(jnp.where((lane > base + i) & (lane < base + SUB), 0.0, row))
            if i + 1 < SUB:
                strip = jnp.where(at & (sub > i), 0.0, strip) - factor * row
        own = jnp.where(lane == base + sub, 1.0, strip)
        result.append(jnp.where(lane <= base + sub, own, 0.0) * lax.rsqrt(pivots))
        inside = (lane >= base) & (lane < base + SUB)
        for q in range(p + 1, count):
            target = strips[q]
            edge = [
                jnp.broadcast_to(target[:, base + j : base + j + 1], (SUB, width))
                for j in range(SUB)
            ]
            target = jnp.where(inside, 0.0, target)
            for i in range(SUB):
                weight = edge[i] * scale[i]
                for j in range(i + 1, SUB):
                    edge[j] = edge[j] - weight * taps[i, j]
                target = target - weight * rows[i]
            strips[q] = target
    return result


def factor_kernel(a_ref, u_ref, inv_ref):
    block = inv_ref.shape[1]
    count = a_ref.shape[0] // block
    u_ref[...] = a_ref[...]

    @pl.loop(0, count)
    def _(k):
        start = pl.multiple_of(k * block, block)
        strips = [
            u_ref[pl.ds(pl.multiple_of(start + s * SUB, SUB), SUB), pl.ds(start, block)]
            for s in range(block // SUB)
        ]
        for s, strip in enumerate(unit_inverse(strips)):
            inv_ref[pl.ds(pl.multiple_of(start + s * SUB, SUB), SUB), :] = strip

        for step in range(count - 1):

            @pl.when(k == step)
            def _():
                here, rest = step * block, (step + 1) * block
                inverse = split(inv_ref[here:rest, :])
                panel = dot3(inverse, split(u_ref[here:rest, rest:]), NN)
                u_ref[here:rest, rest:] = panel
                high, low = split(panel)
                for i in range(step + 1, count):
                    at = (i - step - 1) * block
                    left = (high[:, at : at + block], low[:, at : at + block])
                    u_ref[i * block : (i + 1) * block, i * block :] -= dot3(
                        left, (high[:, at:], low[:, at:]), TN
                    )


def solve_kernel(
    col_count, row_count, u_ref, inv_ref, near_ref, tile_ref, v_ref, noise_ref, *refs
):
    block = inv_ref.shape[1]
    pivots = u_ref.shape[0]
    count = pivots // block
    far_refs = refs[: col_count - 1]
    side_refs = refs[col_count - 1 : col_count + row_count - 2]
    mine_ref, s_ref, x_ref, w_ref, high_ref, low_ref, b_ref = refs[col_count + row_count - 2 :]
    my_col, my_row = lax.axis_index("col"), lax.axis_index("row")
    wide = near_ref.shape[1]
    for shift, piece in enumerate((near_ref, *far_refs)):
        owner = lax.rem(my_col + shift, col_count)
        for a in range(piece.shape[0] // block):
            at = pl.multiple_of((a * col_count + owner) * block, block)
            w_ref[pl.ds(at, block), :wide] = piece[a * block : (a + 1) * block, :]
    for shift, piece in enumerate((mine_ref, *side_refs)):
        owner = lax.rem(my_row + shift, row_count)
        for b in range(piece.shape[1] // block):
            at = pl.multiple_of((b * row_count + owner) * block, block)
            w_ref[pl.ds(at, block), wide:] = piece[:, b * block : (b + 1) * block].T
    rhs = v_ref[...]
    known = []
    for k in range(count):
        here, rest = k * block, (k + 1) * block
        acc = w_ref[here:rest, :]
        part = rhs[:, here:rest]
        if k:
            above = u_ref[:here, here:rest]
            acc = acc - dot3(split(above), (high_ref[:here, :], low_ref[:here, :]), TN)
            part = part - lax.dot_general(
                jnp.concatenate(known, axis=1), above, (NN, ((), ())), precision=HIGH
            )
        inverse = inv_ref[here:rest, :]
        value = dot3(split(inverse), split(acc), NN)
        high, low = split(value)
        high_ref[here:rest, :] = high
        low_ref[here:rest, :] = low
        known.append(lax.dot_general(part, inverse, (NT, ((), ())), precision=HIGH))
    s_ref[...] = tile_ref[...] - dot3(
        (high_ref[:, wide:], low_ref[:, wide:]), (high_ref[:, :wide], low_ref[:, :wide]), TN
    )
    b_ref[...] = noise_ref[...] - jnp.concatenate(known, axis=1)
    for k in reversed(range(count)):
        here, rest = k * block, (k + 1) * block
        part = b_ref[:, here:rest]
        if k + 1 < count:
            part = part - lax.dot_general(
                x_ref[:, rest:], u_ref[here:rest, rest:], (NT, ((), ())), precision=HIGH
            )
        x_ref[:, here:rest] = lax.dot_general(
            part, inv_ref[here:rest, :], (NN, ((), ())), precision=HIGH
        )


def gather_kernel(row_count, col_count, block, piece_ref, v_ref, a_ref, vs_ref, send, recv, vsend, vrecv, own):
    my_row, my_col = lax.axis_index("row"), lax.axis_index("col")
    my_group = lax.axis_index("group")
    peers = [
        (lax.rem(my_row + r, row_count), lax.rem(my_col + c, col_count))
        for r in range(row_count)
        for c in range(col_count)
        if r or c
    ]
    n_a = a_ref.shape[0] // block // col_count
    n_b = a_ref.shape[1] // block // row_count
    barrier = pltpu.get_barrier_semaphore()
    for r, c in peers:
        pl.semaphore_signal(barrier, inc=1, device_id=(my_group, r, c), device_id_type=MESH)
    pl.semaphore_wait(barrier, len(peers))

    def where(a, b):
        i = pl.multiple_of((a * col_count + my_col) * block, block)
        j = pl.multiple_of((b * row_count + my_row) * block, block)
        return a_ref.at[pl.ds(i, block), pl.ds(j, block)]

    def source(a, b):
        return piece_ref.at[a * block : (a + 1) * block, b * block : (b + 1) * block]

    slot = my_row * col_count + my_col
    copies = []
    for n, (r, c) in enumerate(peers):
        copies.append(
            pltpu.make_async_remote_copy(
                src_ref=v_ref, dst_ref=vs_ref.at[slot], send_sem=vsend.at[n],
                recv_sem=vrecv.at[n], device_id=(my_group, r, c), device_id_type=MESH,
            )
        )
    for a in range(n_a):
        for b in range(n_b):
            for n, (r, c) in enumerate(peers):
                copies.append(
                    pltpu.make_async_remote_copy(
                        src_ref=source(a, b), dst_ref=where(a, b), send_sem=send.at[n, a, b],
                        recv_sem=recv.at[n, a, b], device_id=(my_group, r, c), device_id_type=MESH,
                    )
                )
    for copy in copies:
        copy.start()
    locals_ = [pltpu.make_async_copy(v_ref, vs_ref.at[slot], own.at[n_a, 0])]
    for a in range(n_a):
        for b in range(n_b):
            locals_.append(pltpu.make_async_copy(source(a, b), where(a, b), own.at[a, b]))
    for copy in locals_:
        copy.start()
    for copy in locals_:
        copy.wait()
    for copy in copies:
        copy.wait()


def place_kernel(col_target, row_target, top_ref, arrived_ref, out_ref):
    groups, n_a, share, n_m, lanes = arrived_ref.shape
    rows = top_ref.shape[1] // share
    out_ref[...] = top_ref[...]
    for g in range(groups):
        for a in range(n_a):
            ct = col_target[g, a]
            for m in range(n_m):
                at = pl.ds(row_target[g, m], share, stride=rows)
                out_ref[ct, at, :] += arrived_ref[g, a, :, m, :]


def local(child_front, top_front, block_map, pivots, noise, top_sample):
    row_count = lax.axis_size("row")
    col_count = lax.axis_size("col")
    group_count = lax.axis_size("group")
    my_row = lax.axis_index("row")
    my_col = lax.axis_index("col")
    my_group = lax.axis_index("group")
    block = child_front.shape[3]
    pivot_total = noise.shape[1]
    child_cols = child_front.shape[1]
    child_rows = child_front.shape[4]
    tile = child_front.reshape(child_cols * block, child_rows * block)

    def global_index(blocks, stride, position):
        starts = jnp.arange(blocks, dtype=jnp.int32)[:, None] * stride + position
        return (starts * block + jnp.arange(block, dtype=jnp.int32)[None, :]).reshape(-1)

    col_index = global_index(child_cols, col_count, my_col)
    row_index = global_index(child_rows, row_count, my_row)
    live = pivots[0]
    dead_cols = (col_index < pivot_total) & (col_index >= live)
    dead_rows = (row_index < pivot_total) & (row_index >= live)
    keep = jnp.logical_not(dead_cols)[:, None] & jnp.logical_not(dead_rows)[None, :]
    unit = (col_index[:, None] == row_index[None, :]).astype(jnp.float32)
    tile = jnp.where(keep, tile, unit)
    n_col = pivot_total // col_count
    n_row = pivot_total // row_count
    pivot_blocks = pivot_total // block
    col_updates = child_cols - n_col // block
    row_updates = child_rows - n_row // block
    corner = tile[:n_col, :n_row]
    near = tile[:n_col, n_row:]
    mine = tile[n_col:, :n_row]
    last = tile[n_col:, n_row:]
    col_blocks = jnp.arange(col_updates, dtype=jnp.int32) * col_count + my_col
    row_blocks = jnp.arange(row_updates, dtype=jnp.int32) * row_count + my_row
    my_map = lax.dynamic_index_in_dim(block_map, my_group, 0, keepdims=False)
    coupled = jnp.take(
        top_sample.reshape(-1, block), jnp.take(my_map, row_blocks), axis=0
    ).reshape(-1)
    v_part = jnp.sum(near * coupled[None, :], axis=1)
    v_part = jnp.broadcast_to(v_part[None, :], (SUB, n_col))

    n_a, n_b = n_col // block, n_row // block
    peers = row_count * col_count - 1
    full, v_parts = pl.pallas_call(
        functools.partial(gather_kernel, row_count, col_count, block),
        out_shape=(
            jax.ShapeDtypeStruct((pivot_total, pivot_total), jnp.float32),
            jax.ShapeDtypeStruct((peers + 1, SUB, n_col), jnp.float32),
        ),
        in_specs=[VMEM, VMEM],
        out_specs=(VMEM, VMEM),
        scratch_shapes=[
            pltpu.SemaphoreType.DMA((peers, n_a, n_b)),
            pltpu.SemaphoreType.DMA((peers, n_a, n_b)),
            pltpu.SemaphoreType.DMA((peers,)),
            pltpu.SemaphoreType.DMA((peers,)),
            pltpu.SemaphoreType.DMA((n_a + 1, n_b)),
        ],
        compiler_params=pltpu.CompilerParams(collective_id=0, has_side_effects=True),
        name="gather",
    )(corner, v_part)
    v = v_parts.reshape(row_count, col_count, SUB, n_a, block).sum(0)
    v = v.transpose(1, 2, 0, 3).reshape(SUB, pivot_total)

    def shifted(value, axis, count, shift):
        pairs = [((i + shift) % count, i) for i in range(count)]
        return lax.ppermute(value, axis, pairs)

    far = [shifted(near, "col", col_count, s) for s in range(1, col_count)]
    side = [shifted(mine, "row", row_count, s) for s in range(1, row_count)]

    upper, inverse = pl.pallas_call(
        factor_kernel,
        out_shape=(
            jax.ShapeDtypeStruct((pivot_total, pivot_total), jnp.float32),
            jax.ShapeDtypeStruct((pivot_total, block), jnp.float32),
        ),
        in_specs=[VMEM],
        out_specs=(VMEM, VMEM),
        cost_estimate=pl.CostEstimate(
            flops=60 * pivot_total**3, bytes_accessed=8 * pivot_total**2, transcendentals=0
        ),
        name="factor",
    )(full)
    noise8 = jnp.broadcast_to(noise, (SUB, pivot_total))
    wide = near.shape[1] + mine.shape[0]
    schur, solved = pl.pallas_call(
        functools.partial(solve_kernel, col_count, row_count),
        out_shape=(
            jax.ShapeDtypeStruct(last.shape, jnp.float32),
            jax.ShapeDtypeStruct((SUB, pivot_total), jnp.float32),
        ),
        in_specs=[VMEM] * (6 + col_count - 1 + row_count - 1 + 1),
        out_specs=(VMEM, VMEM),
        scratch_shapes=[
            pltpu.VMEM((pivot_total, wide), jnp.float32),
            pltpu.VMEM((pivot_total, wide), jnp.bfloat16),
            pltpu.VMEM((pivot_total, wide), jnp.bfloat16),
            pltpu.VMEM((SUB, pivot_total), jnp.float32),
        ],
        name="forward",
    )(upper, inverse, near, last, v, noise8, *far, *side, mine)

    top_cols = top_front.shape[0]
    share = top_front.shape[3]
    top_rows = top_front.shape[4]
    shares = schur.reshape(col_updates, group_count, share, row_updates, block)
    arrived = lax.all_to_all(shares, "group", split_axis=1, concat_axis=1, tiled=True)
    arrived = arrived.reshape(col_updates, group_count, share, row_updates, block).transpose(
        1, 0, 2, 3, 4
    )
    col_target = jnp.take(block_map, col_blocks, axis=1) // col_count
    row_target = jnp.take(block_map, row_blocks, axis=1) // row_count
    top = top_front.reshape(top_cols, share * top_rows, block)
    top_out = pl.pallas_call(
        place_kernel,
        out_shape=jax.ShapeDtypeStruct(top.shape, jnp.float32),
        in_specs=[SMEM, SMEM, VMEM, VMEM],
        out_specs=VMEM,
        name="place",
    )(col_target, row_target, top, arrived)
    return (top_out.reshape(top_front.shape), solved[:1])


def solution(mesh):
    return jax.shard_map(
        local,
        mesh=mesh,
        in_specs=(
            P("group", None, "col", None, None, "row", None),
            P(None, "col", "group", None, None, "row", None),
            P(),
            P("group"),
            P("group", None),
            P(),
        ),
        out_specs=(P(None, "col", "group", None, None, "row", None), P("group", None)),
        check_vma=False,
    )
```

profile of v0, /device:TPU:0, one launch (start us, length us, event | category | flops | bytes accessed | tf_op | source)
XLA Modules:
  0.0 170.6 jit_solution(4842825022525973128)
XLA Ops:
  0.6 0.0 copy-start
  0.7 0.7 dynamic-slice_bitcast_fusion
  1.4 0.6 gather_fusion.2
  2.1 0.1 add_bitcast_fusion
  2.1 0.1 add_bitcast_fusion.1
  2.9 0.1 and_not_fusion
  2.9 0.1 and_not_fusion.1
  3.0 0.0 copy-done
  3.0 0.6 gather_fusion.3
  3.6 0.1 select_bitcast_fusion
  3.7 2.3 %bitcast_select_fusion = f32[512,1024]{1,0:T(8,128)S(1)} fusion(f32[64,8,8,128]{3,2,1,0:T(8,128)} %bitcast.77, s32[1024]{0:T(1024)S(1)} %add_bitcast_fusion, s32[512]{0:T(512)S(1)} %add_bitcast_fusion.1, pred[1024]{0:T(1024)(128)(4,1)S(1)} %and_not_fusion, pred[512]{0:T(512)(128)(4,1)S(1)} %and_not_fusion.1), kind=kLoop, calls=%fused_computation.4 | loop fusion | flops 2097152 | bytes 4201984 | tf_op jit(solution)/shard_map/jit(_where)/select_n | solution.py:271
  6.0 1.1 fusion.9
  7.1 0.0 copy-start.1
  7.1 0.0 copy-start.2
  7.1 2.4 %collective-permute-start = (f32[256,512]{1,0:T(8,128)S(1)}, f32[256,512]{1,0:T(8,128)S(1)}, u32[]{:S(2)}, u32[]{:S(2)}) collective-permute-start(f32[256,512]{1,0:T(8,128)S(1)} %get-tuple-element.23.near_ref), channel_id=1, source_target_pairs={{1,0},{2,1},{3,2},{0,3},{5,4},{6,5},{7,6},{4,7},{9,8},{10,9},{11,1... | collective-permute-start | bytes 1572872 | tf_op jit(solution)/shard_map/ppermute | solution.py:315
  9.6 0.6 collective-permute-start.1
  10.2 0.2 collective-permute-start.2
  10.4 1.5 collective-permute-start.3
  11.9 0.6 broadcast_in_dim.47.v_ref
  12.4 69.4 %gather.32 = (f32[1024,1024]{1,0:T(8,128)}, f32[8,8,256]{2,1,0:T(8,128)}) custom-call(f32[256,512]{1,0:T(8,128)} %get-tuple-element.24.piece_ref, f32[8,256]{1,0:T(8,128)} %broadcast_in_dim.47.v_ref), custom_call_target="tpu_custom_call" | custom-call | tf_op jit(solution)/shard_map/gather/pallas_call | solution.py:292
  81.9 0.0 copy-start.8
  81.9 0.0 copy-start.9
  81.9 41.1 %factor.1 = (f32[1024,1024]{1,0:T(8,128)}, f32[1024,128]{1,0:T(8,128)}) custom-call(f32[1024,1024]{1,0:T(8,128)} %get-tuple-element.8.a_ref), custom_call_target="tpu_custom_call" | custom-call | flops 64424509440 | bytes 8388608 | tf_op jit(solution)/shard_map/factor/pallas_call | solution.py:320
  123.0 0.0 copy-done.1
  123.0 0.0 copy-done.2
  123.0 0.0 copy-done.8
  123.0 0.6 copy.23
  123.6 0.0 collective-permute-done.refs_0_
  123.6 0.0 copy-start.4
  123.6 0.0 collective-permute-done.1.refs_1_
  123.6 0.0 copy-start.5
  123.7 0.0 collective-permute-done.2.refs_2_
  123.7 0.0 copy-start.6
  123.7 0.0 collective-permute-done.3.refs_3_
  123.7 0.0 copy-start.7
  123.7 0.0 copy-done.9
  123.7 0.7 broadcast_in_dim.49.noise_ref
  124.4 0.0 copy-done.4
  124.4 0.2 copy-done.5
  124.6 0.2 copy-done.6
  124.8 0.2 copy-done.7
  125.0 17.0 %forward.1 = (f32[256,512]{1,0:T(8,128)}, f32[8,1024]{1,0:T(8,128)}) custom-call(f32[1024,1024]{1,0:T(8,128)} %get-tuple-element.9.u_ref, f32[1024,128]{1,0:T(8,128)} %get-tuple-element.10.inv_ref, f32[256,512]{1,0:T(8,128)} %copy-done.2, f32[256,512]{1,0:T(8,128)} %get-tuple-element.22.tile_ref, f32[8,1024]{1,0:T(8,128)} %bitcast.78, ...), custom_call_target="tpu_custom_call" | custom-call | tf_op jit(solution)/shard_map/forward/pallas_call | solution.py:335
  141.9 0.0 copy-start.10
  142.0 1.2 reshape.196
  143.2 0.8 copy.24
  144.0 4.9 %all-to-all-start = ((f32[2,4,32,4,128]{4,3,2,0,1:T(4,128)}), f32[2,4,32,4,128]{4,3,2,0,1:T(4,128)S(1)}, u32[]{:S(2)}, u32[]{:S(2)}) async-start(f32[2,4,32,4,128]{4,3,2,0,1:T(4,128)} %copy.24), calls=%async_computation | async-start | bytes 1048576 | tf_op jit(solution)/shard_map/all_to_all | solution.py:356
  148.9 0.0 copy-done.10
  148.9 0.1 copy.19
  149.0 0.6 gather_fusion.1
  149.5 0.6 gather_fusion
  150.1 0.1 copy.20
  150.2 0.1 copy.22
  150.3 0.6 add_select_fusion.1.col_target
  150.9 0.6 add_select_fusion.row_target
  151.5 1.4 slice.19
  152.9 11.6 %all-to-all-done = f32[2,4,32,4,128]{4,3,2,0,1:T(4,128)S(1)} async-done(((f32[2,4,32,4,128]{4,3,2,0,1:T(4,128)}), f32[2,4,32,4,128]{4,3,2,0,1:T(4,128)S(1)}, u32[]{:S(2)}, u32[]{:S(2)}) %all-to-all-start) | async-done | bytes 524320 | tf_op jit(solution)/shard_map/all_to_all | solution.py:356
  164.5 0.0 copy-start.3
  164.5 0.8 copy-done.3
  165.3 5.4 %place.1 = f32[12,768,128]{2,1,0:T(8,128)} custom-call(s32[4,2]{1,0:T(4,128)} %add_select_fusion.1.col_target, s32[4,4]{1,0:T(4,128)} %add_select_fusion.row_target, f32[12,768,128]{2,1,0:T(8,128)} %bitcast.74, f32[4,2,32,4,128]{4,3,2,1,0:T(4,128)} %bitcast.76), custom_call_target="tpu_custom_call" | custom-call | tf_op jit(solution)/shard_map/place/pallas_call | solution.py:363
  (12 shorter events, 0.1 us)
Async XLA Ops:
  0.6 2.4 %copy-start = (f32[6144]{0:T(1024)S(1)}, f32[6144]{0:T(1024)}, u32[]{:S(2)}) copy-start(f32[6144]{0:T(1024)} %param.11) | copy-start | bytes 73732
  7.1 115.9 %copy-start.1 = (f32[256,512]{1,0:T(8,128)}, f32[256,512]{1,0:T(8,128)S(1)}, u32[]{:S(2)}) copy-start(f32[256,512]{1,0:T(8,128)S(1)} %get-tuple-element.20.refs_4_) | copy-start | bytes 1572868
  7.1 115.9 %copy-start.2 = (f32[256,512]{1,0:T(8,128)}, f32[256,512]{1,0:T(8,128)S(1)}, u32[]{:S(2)}) copy-start(f32[256,512]{1,0:T(8,128)S(1)} %get-tuple-element.23.near_ref) | copy-start | bytes 1572868
  7.1 116.5 %collective-permute-start = (f32[256,512]{1,0:T(8,128)S(1)}, f32[256,512]{1,0:T(8,128)S(1)}, u32[]{:S(2)}, u32[]{:S(2)}) collective-permute-start(f32[256,512]{1,0:T(8,128)S(1)} %get-tuple-element.23.near_ref), channel_id=1, source_target_pairs={{1,0},{2,1},{3,2},{0,3},{5,4},{6,5},{7,6},{4,7},{9,8},{10,9},{11,1... | collective-permute-start | bytes 1572872 | tf_op jit(solution)/shard_map/ppermute | solution.py:315
  9.6 114.1 %collective-permute-start.1 = (f32[256,512]{1,0:T(8,128)S(1)}, f32[256,512]{1,0:T(8,128)S(1)}, u32[]{:S(2)}, u32[]{:S(2)}) collective-permute-start(f32[256,512]{1,0:T(8,128)S(1)} %get-tuple-element.23.near_ref), channel_id=1, source_target_pairs={{2,0},{3,1},{0,2},{1,3},{6,4},{7,5},{4,6},{5,7},{10,8},{11,9},{8,1... | collective-permute-start | bytes 1572872 | tf_op jit(solution)/shard_map/ppermute | solution.py:315
  10.2 113.5 %collective-permute-start.2 = (f32[256,512]{1,0:T(8,128)S(1)}, f32[256,512]{1,0:T(8,128)S(1)}, u32[]{:S(2)}, u32[]{:S(2)}) collective-permute-start(f32[256,512]{1,0:T(8,128)S(1)} %get-tuple-element.23.near_ref), channel_id=1, source_target_pairs={{3,0},{0,1},{1,2},{2,3},{7,4},{4,5},{5,6},{6,7},{11,8},{8,9},{9,10... | collective-permute-start | bytes 1572872 | tf_op jit(solution)/shard_map/ppermute | solution.py:315
  10.4 113.3 %collective-permute-start.3 = (f32[256,512]{1,0:T(8,128)S(1)}, f32[256,512]{1,0:T(8,128)S(1)}, u32[]{:S(2)}, u32[]{:S(2)}) collective-permute-start(f32[256,512]{1,0:T(8,128)S(1)} %get-tuple-element.20.refs_4_), channel_id=1, source_target_pairs={{4,0},{0,4},{5,1},{1,5},{6,2},{2,6},{7,3},{3,7},{12,8},{8,12},{13,... | collective-permute-start | bytes 1572872 | tf_op jit(solution)/shard_map/ppermute | solution.py:315
  81.9 41.1 %copy-start.8 = (f32[8,8,256]{2,1,0:T(8,128)S(1)}, f32[8,8,256]{2,1,0:T(8,128)}, u32[]{:S(2)}) copy-start(f32[8,8,256]{2,1,0:T(8,128)} %get-tuple-element.11) | copy-start | bytes 196612
  81.9 41.8 %copy-start.9 = (f32[1,1024]{1,0:T(1,128)S(1)}, f32[1,1024]{1,0:T(1,128)}, u32[]{:S(2)}) copy-start(f32[1,1024]{1,0:T(1,128)} %param.10) | copy-start | bytes 12292
  123.6 0.8 copy-start.4
  123.6 1.0 copy-start.5
  123.7 1.2 copy-start.6
  123.7 1.3 copy-start.7
  141.9 6.9 %copy-start.10 = (s32[4,8]{1,0:T(4,128)S(1)}, s32[4,8]{1,0:T(4,128)}, u32[]{:S(2)}) copy-start(s32[4,8]{1,0:T(4,128)} %param.8) | copy-start | bytes 388
  144.0 20.5 %all-to-all-start = ((f32[2,4,32,4,128]{4,3,2,0,1:T(4,128)}), f32[2,4,32,4,128]{4,3,2,0,1:T(4,128)S(1)}, u32[]{:S(2)}, u32[]{:S(2)}) async-start(f32[2,4,32,4,128]{4,3,2,0,1:T(4,128)} %copy.24), calls=%async_computation | async-start | bytes 1048576 | tf_op jit(solution)/shard_map/all_to_all | solution.py:356
  164.5 0.8 copy-start.3
where the time goes:
time: 171 us
  Pallas kernels  133 us (78%)
  waiting for transfers between devices  11.6 us (7%)
  local copies, waits for them, and re-layouts  9.98 us (6%)
  starting transfers between devices  9.59 us (6%)
  other arithmetic  5.13 us (3%)
    pallas_call x1, Pallas kernels, local(): pl.pallas_call(functools.partial(gather_kernel, row_count, col_count, blo...  69.4 us
    pallas_call x1, Pallas kernels, local(): pl.pallas_call(factor_kernel, out_shape=(jax.ShapeDtypeStruct((pivot_tota...  41.1 us
    pallas_call x1, Pallas kernels, local(): pl.pallas_call(functools.partial(solve_kernel, col_count, row_count), out...  17 us
    all_to_all x1, waiting for transfers between devices, local(): lax.all_to_all(shares, 'group', split_axis=1, concat_axis=1, tiled=True)  11.6 us
    pallas_call x1, Pallas kernels, local(): pl.pallas_call(place_kernel, out_shape=jax.ShapeDtypeStruct(top.shape, jn...  5.38 us
    all_to_all x1, starting transfers between devices, local(): lax.all_to_all(shares, 'group', split_axis=1, concat_axis=1, tiled=True)  4.87 us
    ppermute x4, starting transfers between devices, shifted(): return lax.ppermute(value, axis, pairs)  4.72 us
  transfers between devices with their start and end apart: 5, of which 1 were waited for; matrix products, arithmetic and copies ran while one was open for 3% of the time, Pallas kernels for 65%

commit v1 on v0

--- a/solution.py
+++ b/solution.py
@@ -92,7 +92,9 @@
 def factor_kernel(a_ref, u_ref, inv_ref):
     block = inv_ref.shape[1]
     count = a_ref.shape[0] // block
-    u_ref[...] = a_ref[...]
+    for i in range(count):
+        rows = slice(i * block, (i + 1) * block)
+        u_ref[rows, i * block :] = a_ref[rows, i * block :]
 
     @pl.loop(0, count)
     def _(k):
@@ -129,7 +131,7 @@
     count = pivots // block
     far_refs = refs[: col_count - 1]
     side_refs = refs[col_count - 1 : col_count + row_count - 2]
-    mine_ref, s_ref, x_ref, w_ref, high_ref, low_ref, b_ref = refs[col_count + row_count - 2 :]
+    mine_ref, s_ref, b_ref, w_ref, high_ref, low_ref = refs[col_count + row_count - 2 :]
     my_col, my_row = lax.axis_index("col"), lax.axis_index("row")
     wide = near_ref.shape[1]
     for shift, piece in enumerate((near_ref, *far_refs)):
@@ -164,6 +166,159 @@
         (high_ref[:, wide:], low_ref[:, wide:]), (high_ref[:, :wide], low_ref[:, :wide]), TN
     )
     b_ref[...] = noise_ref[...] - jnp.concatenate(known, axis=1)
+
+
+def flip(position, bit):
+    return position + bit - 2 * bit * lax.rem(position // bit, 2)
+
+
+def cube_steps(row_count, col_count, turned):
+    rows = [("row", 1 << t) for t in reversed(range(row_count.bit_length() - 1))]
+    cols = [("col", 1 << t) for t in reversed(range(col_count.bit_length() - 1))]
+    return cols[:-1] + rows + cols[-1:] if turned else rows + cols
+
+
+def gather_kernel(row_count, col_count, block, piece_ref, v_ref, a_ref, vs_ref, send, recv, own):
+    my_row, my_col = lax.axis_index("row"), lax.axis_index("col")
+    my_group = lax.axis_index("group")
+    n_a = a_ref.shape[0] // block // col_count
+    n_b = a_ref.shape[1] // block // row_count
+    straight = cube_steps(row_count, col_count, False)
+    turned = cube_steps(row_count, col_count, True)
+    depth = len(straight)
+
+    def moved(step, r, c):
+        return (flip(r, step[1]), c) if step[0] == "row" else (r, flip(c, step[1]))
+
+    barrier = pltpu.get_barrier_semaphore()
+    for step in straight:
+        r, c = moved(step, my_row, my_col)
+        pl.semaphore_signal(barrier, inc=1, device_id=(my_group, r, c), device_id_type=MESH)
+    pl.semaphore_wait(barrier, depth)
+
+    parts = [
+        (a, b, a * n_b + b, turned if b % 2 else straight) for a in range(n_a) for b in range(n_b)
+    ]
+    parts.append((None, None, n_a * n_b, straight))
+
+    def place(part, r, c):
+        a, b, n, _ = part
+        if a is None:
+            return vs_ref.at[r * col_count + c]
+        i = pl.multiple_of((a * col_count + c) * block, block)
+        j = pl.multiple_of((b * row_count + r) * block, block)
+        return a_ref.at[pl.ds(i, block), pl.ds(j, block)]
+
+    def source(part):
+        a, b, n, _ = part
+        if a is None:
+            return v_ref
+        return piece_ref.at[a * block : (a + 1) * block, b * block : (b + 1) * block]
+
+    def guarded(part, r, c, action):
+        a, b, n, _ = part
+        if a is None:
+            action()
+        else:
+            pl.when(a * col_count + c <= b * row_count + r)(action)
+
+    def origin(part, subset):
+        r, c = my_row, my_col
+        for t, step in enumerate(part[3]):
+            if subset >> t & 1:
+                r, c = moved(step, r, c)
+        return r, c
+
+    def copy_of(part, subset, t):
+        spot = place(part, *origin(part, subset))
+        r, c = moved(part[3][t], my_row, my_col)
+        return pltpu.make_async_remote_copy(
+            src_ref=spot if subset else source(part),
+            dst_ref=spot,
+            send_sem=send.at[part[2], subset | 1 << t],
+            recv_sem=recv.at[part[2], subset | 1 << t],
+            device_id=(my_group, r, c),
+            device_id_type=MESH,
+        )
+
+    def steps_after(subset):
+        return range(subset.bit_length(), depth)
+
+    def own_copy(part):
+        return pltpu.make_async_copy(source(part), place(part, my_row, my_col), own.at[part[2]])
+
+    for subset in range(1 << depth):
+        for part in parts:
+
+            def forward():
+                if subset:
+                    top = subset.bit_length() - 1
+                    spot = place(part, *origin(part, subset))
+                    r, c = moved(part[3][top], my_row, my_col)
+                    pltpu.make_async_remote_copy(
+                        src_ref=spot,
+                        dst_ref=spot,
+                        send_sem=send.at[part[2], subset],
+                        recv_sem=recv.at[part[2], subset],
+                        device_id=(my_group, r, c),
+                        device_id_type=MESH,
+                    ).wait_recv()
+                for t in steps_after(subset):
+                    copy_of(part, subset, t).start()
+                if not subset:
+                    own_copy(part).start()
+
+            guarded(part, *origin(part, subset), forward)
+    for subset in range(1 << depth):
+        for part in parts:
+
+            def finish():
+                for t in steps_after(subset):
+                    copy_of(part, subset, t).wait_send()
+                if not subset:
+                    own_copy(part).wait()
+
+            guarded(part, *origin(part, subset), finish)
+
+
+def exchange_kernel(share, s_ref, u_ref, inv_ref, b_ref, out_ref, x_ref, send, recv, own):
+    block = inv_ref.shape[1]
+    count = u_ref.shape[0] // block
+    groups, n_a = out_ref.shape[0], out_ref.shape[1]
+    my_row, my_col = lax.axis_index("row"), lax.axis_index("col")
+    me = lax.axis_index("group")
+    barrier = pltpu.get_barrier_semaphore()
+    for d in range(1, groups):
+        pl.semaphore_signal(
+            barrier,
+            inc=1,
+            device_id=(lax.rem(me + d, groups), my_row, my_col),
+            device_id_type=MESH,
+        )
+    pl.semaphore_wait(barrier, groups - 1)
+
+    def source(g, a):
+        at = pl.multiple_of(a * block + g * share, share)
+        return s_ref.at[pl.ds(at, share), :]
+
+    copies = []
+    for d in range(1, groups):
+        other = lax.rem(me + d, groups)
+        for a in range(n_a):
+            copies.append(
+                pltpu.make_async_remote_copy(
+                    src_ref=source(other, a),
+                    dst_ref=out_ref.at[me, a],
+                    send_sem=send.at[d, a],
+                    recv_sem=recv.at[d, a],
+                    device_id=(other, my_row, my_col),
+                    device_id_type=MESH,
+                )
+            )
+    for a in range(n_a):
+        copies.append(pltpu.make_async_copy(source(me, a), out_ref.at[me, a], own.at[a]))
+    for copy in copies:
+        copy.start()
     for k in reversed(range(count)):
         here, rest = k * block, (k + 1) * block
         part = b_ref[:, here:rest]
@@ -174,74 +329,23 @@
         x_ref[:, here:rest] = lax.dot_general(
             part, inv_ref[here:rest, :], (NN, ((), ())), precision=HIGH
         )
-
-
-def gather_kernel(row_count, col_count, block, piece_ref, v_ref, a_ref, vs_ref, send, recv, vsend, vrecv, own):
-    my_row, my_col = lax.axis_index("row"), lax.axis_index("col")
-    my_group = lax.axis_index("group")
-    peers = [
-        (lax.rem(my_row + r, row_count), lax.rem(my_col + c, col_count))
-        for r in range(row_count)
-        for c in range(col_count)
-        if r or c
-    ]
-    n_a = a_ref.shape[0] // block // col_count
-    n_b = a_ref.shape[1] // block // row_count
-    barrier = pltpu.get_barrier_semaphore()
-    for r, c in peers:
-        pl.semaphore_signal(barrier, inc=1, device_id=(my_group, r, c), device_id_type=MESH)
-    pl.semaphore_wait(barrier, len(peers))
-
-    def where(a, b):
-        i = pl.multiple_of((a * col_count + my_col) * block, block)
-        j = pl.multiple_of((b * row_count + my_row) * block, block)
-        return a_ref.at[pl.ds(i, block), pl.ds(j, block)]
-
-    def source(a, b):
-        return piece_ref.at[a * block : (a + 1) * block, b * block : (b + 1) * block]
-
-    slot = my_row * col_count + my_col
-    copies = []
-    for n, (r, c) in enumerate(peers):
-        copies.append(
-            pltpu.make_async_remote_copy(
-                src_ref=v_ref, dst_ref=vs_ref.at[slot], send_sem=vsend.at[n],
-                recv_sem=vrecv.at[n], device_id=(my_group, r, c), device_id_type=MESH,
-            )
-        )
-    for a in range(n_a):
-        for b in range(n_b):
-            for n, (r, c) in enumerate(peers):
-                copies.append(
-                    pltpu.make_async_remote_copy(
-                        src_ref=source(a, b), dst_ref=where(a, b), send_sem=send.at[n, a, b],
-                        recv_sem=recv.at[n, a, b], device_id=(my_group, r, c), device_id_type=MESH,
-                    )
-                )
-    for copy in copies:
-        copy.start()
-    locals_ = [pltpu.make_async_copy(v_ref, vs_ref.at[slot], own.at[n_a, 0])]
-    for a in range(n_a):
-        for b in range(n_b):
-            locals_.append(pltpu.make_async_copy(source(a, b), where(a, b), own.at[a, b]))
-    for copy in locals_:
-        copy.start()
-    for copy in locals_:
-        copy.wait()
     for copy in copies:
         copy.wait()
 
 
-def place_kernel(col_target, row_target, top_ref, arrived_ref, out_ref):
-    groups, n_a, share, n_m, lanes = arrived_ref.shape
+def place_kernel(col_count, row_count, share, map_ref, top_ref, arrived_ref, out_ref):
+    groups, n_a = arrived_ref.shape[0], arrived_ref.shape[1]
+    lanes = top_ref.shape[2]
     rows = top_ref.shape[1] // share
+    my_row, my_col = lax.axis_index("row"), lax.axis_index("col")
     out_ref[...] = top_ref[...]
     for g in range(groups):
         for a in range(n_a):
-            ct = col_target[g, a]
-            for m in range(n_m):
-                at = pl.ds(row_target[g, m], share, stride=rows)
-                out_ref[ct, at, :] += arrived_ref[g, a, :, m, :]
+            ct = map_ref[g, a * col_count + my_col] // col_count
+            for m in range(arrived_ref.shape[3] // lanes):
+                rt = map_ref[g, m * row_count + my_row] // row_count
+                at = pl.ds(rt, share, stride=rows)
+                out_ref[ct, at, :] += arrived_ref[g, a, :, m * lanes : (m + 1) * lanes]
 
 
 def local(child_front, top_front, block_map, pivots, noise, top_sample):
@@ -278,7 +382,6 @@
     near = tile[:n_col, n_row:]
     mine = tile[n_col:, :n_row]
     last = tile[n_col:, n_row:]
-    col_blocks = jnp.arange(col_updates, dtype=jnp.int32) * col_count + my_col
     row_blocks = jnp.arange(row_updates, dtype=jnp.int32) * row_count + my_row
     my_map = lax.dynamic_index_in_dim(block_map, my_group, 0, keepdims=False)
     coupled = jnp.take(
@@ -298,11 +401,9 @@
         in_specs=[VMEM, VMEM],
         out_specs=(VMEM, VMEM),
         scratch_shapes=[
-            pltpu.SemaphoreType.DMA((peers, n_a, n_b)),
-            pltpu.SemaphoreType.DMA((peers, n_a, n_b)),
-            pltpu.SemaphoreType.DMA((peers,)),
-            pltpu.SemaphoreType.DMA((peers,)),
-            pltpu.SemaphoreType.DMA((n_a + 1, n_b)),
+            pltpu.SemaphoreType.DMA((n_a * n_b + 1, peers + 1)),
+            pltpu.SemaphoreType.DMA((n_a * n_b + 1, peers + 1)),
+            pltpu.SemaphoreType.DMA((n_a * n_b + 1,)),
         ],
         compiler_params=pltpu.CompilerParams(collective_id=0, has_side_effects=True),
         name="gather",
@@ -310,12 +411,14 @@
     v = v_parts.reshape(row_count, col_count, SUB, n_a, block).sum(0)
     v = v.transpose(1, 2, 0, 3).reshape(SUB, pivot_total)
 
+    full, near_later, mine_later = lax.optimization_barrier((full, near, mine))
+
     def shifted(value, axis, count, shift):
         pairs = [((i + shift) % count, i) for i in range(count)]
         return lax.ppermute(value, axis, pairs)
 
-    far = [shifted(near, "col", col_count, s) for s in range(1, col_count)]
-    side = [shifted(mine, "row", row_count, s) for s in range(1, row_count)]
+    far = [shifted(near_later, "col", col_count, s) for s in range(1, col_count)]
+    side = [shifted(mine_later, "row", row_count, s) for s in range(1, row_count)]
 
     upper, inverse = pl.pallas_call(
         factor_kernel,
@@ -332,7 +435,7 @@
     )(full)
     noise8 = jnp.broadcast_to(noise, (SUB, pivot_total))
     wide = near.shape[1] + mine.shape[0]
-    schur, solved = pl.pallas_call(
+    schur, rhs = pl.pallas_call(
         functools.partial(solve_kernel, col_count, row_count),
         out_shape=(
             jax.ShapeDtypeStruct(last.shape, jnp.float32),
@@ -344,7 +447,6 @@
             pltpu.VMEM((pivot_total, wide), jnp.float32),
             pltpu.VMEM((pivot_total, wide), jnp.bfloat16),
             pltpu.VMEM((pivot_total, wide), jnp.bfloat16),
-            pltpu.VMEM((SUB, pivot_total), jnp.float32),
         ],
         name="forward",
     )(upper, inverse, near, last, v, noise8, *far, *side, mine)
@@ -352,21 +454,32 @@
     top_cols = top_front.shape[0]
     share = top_front.shape[3]
     top_rows = top_front.shape[4]
-    shares = schur.reshape(col_updates, group_count, share, row_updates, block)
-    arrived = lax.all_to_all(shares, "group", split_axis=1, concat_axis=1, tiled=True)
-    arrived = arrived.reshape(col_updates, group_count, share, row_updates, block).transpose(
-        1, 0, 2, 3, 4
-    )
-    col_target = jnp.take(block_map, col_blocks, axis=1) // col_count
-    row_target = jnp.take(block_map, row_blocks, axis=1) // row_count
+    arrived, solved = pl.pallas_call(
+        functools.partial(exchange_kernel, share),
+        out_shape=(
+            jax.ShapeDtypeStruct(
+                (group_count, col_updates, share, row_updates * block), jnp.float32
+            ),
+            jax.ShapeDtypeStruct((SUB, pivot_total), jnp.float32),
+        ),
+        in_specs=[VMEM] * 4,
+        out_specs=(VMEM, VMEM),
+        scratch_shapes=[
+            pltpu.SemaphoreType.DMA((group_count, col_updates)),
+            pltpu.SemaphoreType.DMA((group_count, col_updates)),
+            pltpu.SemaphoreType.DMA((col_updates,)),
+        ],
+        compiler_params=pltpu.CompilerParams(collective_id=1, has_side_effects=True),
+        name="exchange",
+    )(schur, upper, inverse, rhs)
     top = top_front.reshape(top_cols, share * top_rows, block)
     top_out = pl.pallas_call(
-        place_kernel,
+        functools.partial(place_kernel, col_count, row_count, share),
         out_shape=jax.ShapeDtypeStruct(top.shape, jnp.float32),
-        in_specs=[SMEM, SMEM, VMEM, VMEM],
+        in_specs=[SMEM, VMEM, VMEM],
         out_specs=VMEM,
         name="place",
-    )(col_target, row_target, top, arrived)
+    )(block_map, top, arrived)
     return (top_out.reshape(top_front.shape), solved[:1])
 
 

time: 171 us -> 112 us (0.65)
  Pallas kernels: 133 us -> 97.1 us
  waiting for transfers between devices: 11.6 us -> 0.01 us
  starting transfers between devices: 9.59 us -> 2.31 us
  local copies, waits for them, and re-layouts: 9.98 us -> 5.83 us
    pallas_call x1, Pallas kernels: 69.4 us -> 23 us  [local(): pl.pallas_call(functools.partial(gather_kernel, row_count, col_count, blo...]
    pallas_call x1 -> x2, Pallas kernels: 5.38 us -> 21.5 us  [the longest x1 16.2 us: local(): pl.pallas_call(functools.partial(exchange_kernel, share), out_shape=(jax....]
    all_to_all x1 -> x0, waiting for transfers between devices: 11.6 us -> none  [local(): lax.all_to_all(shares, 'group', split_axis=1, concat_axis=1, tiled=True)]
    pallas_call x1, Pallas kernels: 17 us -> 11.7 us  [local(): pl.pallas_call(functools.partial(solve_kernel, col_count, row_count), out...]
    all_to_all x1 -> x0, starting transfers between devices: 4.87 us -> none  [local(): lax.all_to_all(shares, 'group', split_axis=1, concat_axis=1, tiled=True)]
    ppermute x4, starting transfers between devices: 4.72 us -> 2.31 us  [shifted(): return lax.ppermute(value, axis, pairs)]
    reshape x2 -> x0, local copies, waits for them, and re-layouts: 2.05 us -> none  [local(): shares = schur.reshape(col_updates, group_count, share, row_updates, block)]
  transfers between devices with their start and end apart: 5 -> 4, of which waited for: 1 -> 0; matrix products, arithmetic and copies ran while one was open for 3% -> 1% of each run, Pallas kernels for 65% -> 37%
where the time goes in v1:
time: 112 us; the launch traced here: 111 us
  Pallas kernels  97.1 us (87%)
  local copies, waits for them, and re-layouts  5.83 us (5%)
  other arithmetic  3.9 us (3%)
  starting transfers between devices  2.31 us (2%)
  between operations  1.45 us (1%)
    pallas_call x1, Pallas kernels, local(): pl.pallas_call(factor_kernel, out_shape=(jax.ShapeDtypeStruct((pivot_tota...  41 us
    pallas_call x1, Pallas kernels, local(): pl.pallas_call(functools.partial(gather_kernel, row_count, col_count, blo...  23 us
    pallas_call x1, Pallas kernels, local(): pl.pallas_call(functools.partial(exchange_kernel, share), out_shape=(jax....  16.2 us
    pallas_call x1, Pallas kernels, local(): pl.pallas_call(functools.partial(solve_kernel, col_count, row_count), out...  11.7 us
    pallas_call x1, Pallas kernels, local(): pl.pallas_call(functools.partial(place_kernel, col_count, row_count, shar...  5.26 us
    select_n x1, other arithmetic, local(): tile = jnp.where(keep, tile, unit)  2.33 us
    ppermute x4, starting transfers between devices, shifted(): return lax.ppermute(value, axis, pairs)  2.31 us
  transfers between devices with their start and end apart: 4, of which 0 were waited for; matrix products, arithmetic and copies ran while one was open for 1% of the time, Pallas kernels for 37%

profile of v1, /device:TPU:0, one launch (start us, length us, event | category | flops | bytes accessed | tf_op | source)
XLA Modules:
  0.0 110.6 jit_solution(15867156754590981098)
XLA Ops:
  0.6 0.0 copy-start
  0.7 0.7 dynamic-slice_bitcast_fusion
  1.4 0.6 gather_fusion
  2.7 0.1 add_bitcast_fusion.1
  2.8 0.1 and_not_fusion.1
  2.9 0.1 add_bitcast_fusion
  2.9 0.1 and_not_fusion
  3.0 0.0 copy-done
  3.0 0.6 gather_fusion.1
  3.6 0.1 select_bitcast_fusion
  3.7 2.3 %bitcast_select_fusion = f32[512,1024]{1,0:T(8,128)S(1)} fusion(f32[64,8,8,128]{3,2,1,0:T(8,128)} %bitcast.41, s32[1024]{0:T(1024)S(1)} %add_bitcast_fusion, s32[512]{0:T(512)S(1)} %add_bitcast_fusion.1, pred[1024]{0:T(1024)(128)(4,1)S(1)} %and_not_fusion, pred[512]{0:T(512)(128)(4,1)S(1)} %and_not_fusion.1), kind=kLoop, calls=%fused_computation.2 | loop fusion | flops 2097152 | bytes 4201984 | tf_op jit(solution)/shard_map/jit(_where)/select_n | solution.py:375
  6.0 1.1 %fusion.2 = (f32[256,512]{1,0:T(8,128)}, f32[256]{0:T(256)S(1)}, f32[256,512]{1,0:T(8,128)S(1)}, f32[256,512]{1,0:T(8,128)S(1)}, f32[256,512]{1,0:T(8,128)}) fusion(f32[512,1024]{1,0:T(8,128)S(1)} %bitcast_select_fusion, f32[512]{0:T(512)S(1)} %select_bitcast_fusion), kind=kLoop, calls=%fused_computation.23 | loop fusion | flops 261888 | bytes 4197376 | tf_op jit(solution)/shard_map/slice | solution.py:384
  7.1 0.0 copy-start.1
  7.1 0.0 copy-start.2
  7.1 0.6 broadcast_in_dim.20.v_ref
  7.8 23.0 %gather.18 = (f32[1024,1024]{1,0:T(8,128)}, f32[8,8,256]{2,1,0:T(8,128)}) custom-call(f32[256,512]{1,0:T(8,128)} %get-tuple-element.34.piece_ref, f32[8,256]{1,0:T(8,128)} %broadcast_in_dim.20.v_ref), custom_call_target="tpu_custom_call" | custom-call | tf_op jit(solution)/shard_map/gather/pallas_call | solution.py:395
  30.8 0.0 copy-start.7
  30.8 0.0 copy-start.8
  30.8 0.5 collective-permute-start.2
  31.3 0.7 collective-permute-start.1
  32.1 1.0 collective-permute-start
  33.1 0.0 collective-permute-start.3
  33.1 41.0 %factor.1 = (f32[1024,1024]{1,0:T(8,128)}, f32[1024,128]{1,0:T(8,128)}) custom-call(f32[1024,1024]{1,0:T(8,128)} %get-tuple-element.14.a_ref), custom_call_target="tpu_custom_call" | custom-call | flops 64424509440 | bytes 8388608 | tf_op jit(solution)/shard_map/factor/pallas_call | solution.py:423
  74.1 0.0 copy-done.1
  74.1 0.0 copy-done.2
  74.1 0.0 copy-done.7
  74.1 0.6 copy.10
  74.7 0.0 collective-permute-done.3.refs_3_
  74.7 0.0 copy-start.6
  74.7 0.0 collective-permute-done.2.refs_2_
  74.7 0.0 copy-start.3
  74.7 0.0 collective-permute-done.1.refs_1_
  74.8 0.0 copy-start.4
  74.8 0.0 collective-permute-done.refs_0_
  74.8 0.0 copy-start.5
  74.8 0.0 copy-done.8
  74.8 0.7 broadcast_in_dim.35.noise_ref
  75.5 0.0 copy-done.6
  75.5 0.2 copy-done.3
  75.7 0.2 copy-done.4
  75.9 0.2 copy-done.5
  76.1 11.7 %forward.1 = (f32[256,512]{1,0:T(8,128)}, f32[8,1024]{1,0:T(8,128)}) custom-call(f32[1024,1024]{1,0:T(8,128)} %get-tuple-element.15.u_ref, f32[1024,128]{1,0:T(8,128)} %get-tuple-element.16.inv_ref, f32[256,512]{1,0:T(8,128)} %copy-done.2, f32[256,512]{1,0:T(8,128)} %get-tuple-element.30.tile_ref, f32[8,1024]{1,0:T(8,128)} %bitcast.42, ...), custom_call_target="tpu_custom_call" | custom-call | tf_op jit(solution)/shard_map/forward/pallas_call | solution.py:438
  87.8 16.2 %exchange.1 = (f32[4,2,32,512]{3,2,1,0:T(8,128)}, f32[8,1024]{1,0:T(8,128)}) custom-call(f32[256,512]{1,0:T(8,128)} %get-tuple-element.20.s_ref, f32[1024,1024]{1,0:T(8,128)} %get-tuple-element.15.u_ref, f32[1024,128]{1,0:T(8,128)} %get-tuple-element.16.inv_ref, f32[8,1024]{1,0:T(8,128)} %get-tuple-element.21.b_ref), custom_call_target="tpu_custom_call" | custom-call | tf_op jit(solution)/shard_map/exchange/pallas_call | solution.py:457
  104.0 1.4 %slice.19 = f32[1,1024]{1,0:T(1,128)} slice(f32[8,1024]{1,0:T(8,128)} %get-tuple-element.23), slice={[0:1], [0:1024]} | slice | bytes 8192 | tf_op jit(solution)/shard_map/slice | solution.py:483
  105.4 5.3 %place.1 = f32[12,768,128]{2,1,0:T(8,128)} custom-call(s32[4,8]{1,0:T(4,128)} %map_ref.1, f32[12,768,128]{2,1,0:T(8,128)} %bitcast.39, f32[4,2,32,512]{3,2,1,0:T(8,128)} %get-tuple-element.22.arrived_ref), custom_call_target="tpu_custom_call" | custom-call | tf_op jit(solution)/shard_map/place/pallas_call | solution.py:476
  (8 shorter events, 0.1 us)
Async XLA Ops:
  0.6 2.4 %copy-start = (f32[6144]{0:T(1024)S(1)}, f32[6144]{0:T(1024)}, u32[]{:S(2)}) copy-start(f32[6144]{0:T(1024)} %param.11) | copy-start | bytes 73732
  7.1 66.9 %copy-start.1 = (f32[256,512]{1,0:T(8,128)}, f32[256,512]{1,0:T(8,128)S(1)}, u32[]{:S(2)}) copy-start(f32[256,512]{1,0:T(8,128)S(1)} %get-tuple-element.19.refs_4_) | copy-start | bytes 1572868
  7.1 66.9 %copy-start.2 = (f32[256,512]{1,0:T(8,128)}, f32[256,512]{1,0:T(8,128)S(1)}, u32[]{:S(2)}) copy-start(f32[256,512]{1,0:T(8,128)S(1)} %get-tuple-element.18.near_ref) | copy-start | bytes 1572868
  30.8 43.3 %copy-start.7 = (f32[8,8,256]{2,1,0:T(8,128)S(1)}, f32[8,8,256]{2,1,0:T(8,128)}, u32[]{:S(2)}) copy-start(f32[8,8,256]{2,1,0:T(8,128)} %get-tuple-element.17) | copy-start | bytes 196612
  30.8 44.0 %copy-start.8 = (f32[1,1024]{1,0:T(1,128)S(1)}, f32[1,1024]{1,0:T(1,128)}, u32[]{:S(2)}) copy-start(f32[1,1024]{1,0:T(1,128)} %param.10) | copy-start | bytes 12292
  30.8 43.9 %collective-permute-start.2 = (f32[256,512]{1,0:T(8,128)S(1)}, f32[256,512]{1,0:T(8,128)S(1)}, u32[]{:S(2)}, u32[]{:S(2)}) collective-permute-start(f32[256,512]{1,0:T(8,128)S(1)} %get-tuple-element.18.near_ref), channel_id=1, source_target_pairs={{3,0},{0,1},{1,2},{2,3},{7,4},{4,5},{5,6},{6,7},{11,8},{8,9},{9,10... | collective-permute-start | bytes 1572872 | tf_op jit(solution)/shard_map/ppermute | solution.py:418
  31.3 43.4 %collective-permute-start.1 = (f32[256,512]{1,0:T(8,128)S(1)}, f32[256,512]{1,0:T(8,128)S(1)}, u32[]{:S(2)}, u32[]{:S(2)}) collective-permute-start(f32[256,512]{1,0:T(8,128)S(1)} %get-tuple-element.18.near_ref), channel_id=1, source_target_pairs={{2,0},{3,1},{0,2},{1,3},{6,4},{7,5},{4,6},{5,7},{10,8},{11,9},{8,1... | collective-permute-start | bytes 1572872 | tf_op jit(solution)/shard_map/ppermute | solution.py:418
  32.1 42.7 %collective-permute-start = (f32[256,512]{1,0:T(8,128)S(1)}, f32[256,512]{1,0:T(8,128)S(1)}, u32[]{:S(2)}, u32[]{:S(2)}) collective-permute-start(f32[256,512]{1,0:T(8,128)S(1)} %get-tuple-element.18.near_ref), channel_id=1, source_target_pairs={{1,0},{2,1},{3,2},{0,3},{5,4},{6,5},{7,6},{4,7},{9,8},{10,9},{11,1... | collective-permute-start | bytes 1572872 | tf_op jit(solution)/shard_map/ppermute | solution.py:418
  33.1 41.6 %collective-permute-start.3 = (f32[256,512]{1,0:T(8,128)S(1)}, f32[256,512]{1,0:T(8,128)S(1)}, u32[]{:S(2)}, u32[]{:S(2)}) collective-permute-start(f32[256,512]{1,0:T(8,128)S(1)} %get-tuple-element.19.refs_4_), channel_id=1, source_target_pairs={{4,0},{0,4},{5,1},{1,5},{6,2},{2,6},{7,3},{3,7},{12,8},{8,12},{13,... | collective-permute-start | bytes 1572872 | tf_op jit(solution)/shard_map/ppermute | solution.py:418
  74.7 0.8 copy-start.6
  74.7 1.0 copy-start.3
  74.8 1.2 %copy-start.4 = (f32[256,512]{1,0:T(8,128)}, f32[256,512]{1,0:T(8,128)S(1)}, u32[]{:S(2)}) copy-start(f32[256,512]{1,0:T(8,128)S(1)} %collective-permute-done.1.refs_1_) | copy-start | bytes 1572868
  74.8 1.3 %copy-start.5 = (f32[256,512]{1,0:T(8,128)}, f32[256,512]{1,0:T(8,128)S(1)}, u32[]{:S(2)}) copy-start(f32[256,512]{1,0:T(8,128)S(1)} %collective-permute-done.refs_0_) | copy-start | bytes 1572868

commit v2 on v1

--- a/solution.py
+++ b/solution.py
@@ -1,5 +1,4 @@
 import functools
-import math
 
 import jax
 import jax.numpy as jnp
@@ -9,7 +8,6 @@
 from jax.sharding import PartitionSpec as P
 
 MESH = pl.DeviceIdType.MESH
-HIGH = lax.Precision.HIGHEST
 SUB = 8
 VMEM = pl.BlockSpec(memory_space=pltpu.VMEM)
 SMEM = pl.BlockSpec(memory_space=pltpu.SMEM)
@@ -153,15 +151,13 @@
         if k:
             above = u_ref[:here, here:rest]
             acc = acc - dot3(split(above), (high_ref[:here, :], low_ref[:here, :]), TN)
-            part = part - lax.dot_general(
-                jnp.concatenate(known, axis=1), above, (NN, ((), ())), precision=HIGH
-            )
+            part = part - dot3(split(jnp.concatenate(known, axis=1)), split(above), NN)
         inverse = inv_ref[here:rest, :]
         value = dot3(split(inverse), split(acc), NN)
         high, low = split(value)
         high_ref[here:rest, :] = high
         low_ref[here:rest, :] = low
-        known.append(lax.dot_general(part, inverse, (NT, ((), ())), precision=HIGH))
+        known.append(dot3(split(part), split(inverse), NT))
     s_ref[...] = tile_ref[...] - dot3(
         (high_ref[:, wide:], low_ref[:, wide:]), (high_ref[:, :wide], low_ref[:, :wide]), TN
     )
@@ -319,33 +315,41 @@
         copies.append(pltpu.make_async_copy(source(me, a), out_ref.at[me, a], own.at[a]))
     for copy in copies:
         copy.start()
+    solved = {}
     for k in reversed(range(count)):
         here, rest = k * block, (k + 1) * block
         part = b_ref[:, here:rest]
+        if k + 2 < count:
+            early = jnp.concatenate([solved[n] for n in range(k + 2, count)], axis=1)
+            part = part - dot3(split(early), split(u_ref[here:rest, rest + block :]), NT)
         if k + 1 < count:
-            part = part - lax.dot_general(
-                x_ref[:, rest:], u_ref[here:rest, rest:], (NT, ((), ())), precision=HIGH
-            )
-        x_ref[:, here:rest] = lax.dot_general(
-            part, inv_ref[here:rest, :], (NN, ((), ())), precision=HIGH
-        )
+            weights = split(u_ref[here:rest, rest : rest + block])
+            part = part - dot3(split(solved[k + 1]), weights, NT)
+        solved[k] = dot3(split(part), split(inv_ref[here:rest, :]), NN)
+        x_ref[:, here:rest] = solved[k]
     for copy in copies:
         copy.wait()
 
 
-def place_kernel(col_count, row_count, share, map_ref, top_ref, arrived_ref, out_ref):
+def place_kernel(
+    col_count, row_count, share, map_ref, top_ref, arrived_ref, sample_ref, out_ref, x_ref
+):
     groups, n_a = arrived_ref.shape[0], arrived_ref.shape[1]
     lanes = top_ref.shape[2]
     rows = top_ref.shape[1] // share
     my_row, my_col = lax.axis_index("row"), lax.axis_index("col")
+    here = pl.program_id(0)
     out_ref[...] = top_ref[...]
+    x_ref[...] = sample_ref[:1, :]
     for g in range(groups):
         for a in range(n_a):
-            ct = map_ref[g, a * col_count + my_col] // col_count
-            for m in range(arrived_ref.shape[3] // lanes):
-                rt = map_ref[g, m * row_count + my_row] // row_count
-                at = pl.ds(rt, share, stride=rows)
-                out_ref[ct, at, :] += arrived_ref[g, a, :, m * lanes : (m + 1) * lanes]
+
+            @pl.when(map_ref[g, a * col_count + my_col] // col_count == here)
+            def _():
+                for m in range(arrived_ref.shape[3] // lanes):
+                    rt = map_ref[g, m * row_count + my_row] // row_count
+                    at = pl.ds(rt, share, stride=rows)
+                    out_ref[0, at, :] += arrived_ref[g, a, :, m * lanes : (m + 1) * lanes]
 
 
 def local(child_front, top_front, block_map, pivots, noise, top_sample):
@@ -473,14 +477,19 @@
         name="exchange",
     )(schur, upper, inverse, rhs)
     top = top_front.reshape(top_cols, share * top_rows, block)
-    top_out = pl.pallas_call(
+    column = pl.BlockSpec((1, share * top_rows, block), lambda n: (n, 0, 0))
+    top_out, sample = pl.pallas_call(
         functools.partial(place_kernel, col_count, row_count, share),
-        out_shape=jax.ShapeDtypeStruct(top.shape, jnp.float32),
-        in_specs=[SMEM, VMEM, VMEM],
-        out_specs=VMEM,
+        grid=(top_cols,),
+        out_shape=(
+            jax.ShapeDtypeStruct(top.shape, jnp.float32),
+            jax.ShapeDtypeStruct((1, pivot_total), jnp.float32),
+        ),
+        in_specs=[SMEM, column, VMEM, VMEM],
+        out_specs=(column, VMEM),
         name="place",
-    )(block_map, top, arrived)
-    return (top_out.reshape(top_front.shape), solved[:1])
+    )(block_map, top, arrived, solved)
+    return (top_out.reshape(top_front.shape), sample)
 
 
 def solution(mesh):

time: 112 us -> 114 us (1.018)
  Pallas kernels: 97.1 us -> 101 us
  local copies, waits for them, and re-layouts: 5.83 us -> 4.44 us
    pallas_call x1, Pallas kernels: 5.26 us -> 9.62 us  [local(): pl.pallas_call(functools.partial(place_kernel, col_count, row_count, shar...]
    slice x1 -> x0, local copies, waits for them, and re-layouts: 1.35 us -> none  [local(): return (top_out.reshape(top_front.shape), solved[:1])]
  transfers between devices with their start and end apart: 4 -> 4, of which waited for: 0 -> 0; matrix products, arithmetic and copies ran while one was open for 1% -> 1% of each run, Pallas kernels for 37% -> 36%
where the time goes in v2:
time: 114 us; the launch traced here: 113 us
  Pallas kernels  101 us (89%)
  local copies, waits for them, and re-layouts  4.44 us (4%)
  other arithmetic  3.9 us (3%)
  starting transfers between devices  2.31 us (2%)
  between operations  1.45 us (1%)
    pallas_call x1, Pallas kernels, local(): pl.pallas_call(factor_kernel, out_shape=(jax.ShapeDtypeStruct((pivot_tota...  40.9 us
    pallas_call x1, Pallas kernels, local(): pl.pallas_call(functools.partial(gather_kernel, row_count, col_count, blo...  23 us
    pallas_call x1, Pallas kernels, local(): pl.pallas_call(functools.partial(exchange_kernel, share), out_shape=(jax....  16.2 us
    pallas_call x1, Pallas kernels, local(): pl.pallas_call(functools.partial(solve_kernel, col_count, row_count), out...  11.4 us
    pallas_call x1, Pallas kernels, local(): pl.pallas_call(functools.partial(place_kernel, col_count, row_count, shar...  9.62 us
    select_n x1, other arithmetic, local(): tile = jnp.where(keep, tile, unit)  2.33 us
    ppermute x4, starting transfers between devices, shifted(): return lax.ppermute(value, axis, pairs)  2.31 us
  transfers between devices with their start and end apart: 4, of which 0 were waited for; matrix products, arithmetic and copies ran while one was open for 1% of the time, Pallas kernels for 36%

profile of v2, /device:TPU:0, one launch (start us, length us, event | category | flops | bytes accessed | tf_op | source)
XLA Modules:
  0.0 113.3 jit_solution(14737943196273775101)
XLA Ops:
  0.6 0.0 copy-start
  0.7 0.7 dynamic-slice_bitcast_fusion
  1.4 0.6 gather_fusion
  2.7 0.1 add_bitcast_fusion.1
  2.8 0.1 and_not_fusion.1
  2.9 0.1 add_bitcast_fusion
  2.9 0.1 and_not_fusion
  3.0 0.0 copy-done
  3.0 0.6 gather_fusion.1
  3.6 0.1 select_bitcast_fusion
  3.7 2.3 %bitcast_select_fusion = f32[512,1024]{1,0:T(8,128)S(1)} fusion(f32[64,8,8,128]{3,2,1,0:T(8,128)} %bitcast.40, s32[1024]{0:T(1024)S(1)} %add_bitcast_fusion, s32[512]{0:T(512)S(1)} %add_bitcast_fusion.1, pred[1024]{0:T(1024)(128)(4,1)S(1)} %and_not_fusion, pred[512]{0:T(512)(128)(4,1)S(1)} %and_not_fusion.1), kind=kLoop, calls=%fused_computation.2 | loop fusion | flops 2097152 | bytes 4201984 | tf_op jit(solution)/shard_map/jit(_where)/select_n | solution.py:379
  6.0 1.1 %fusion.2 = (f32[256,512]{1,0:T(8,128)}, f32[256]{0:T(256)S(1)}, f32[256,512]{1,0:T(8,128)S(1)}, f32[256,512]{1,0:T(8,128)S(1)}, f32[256,512]{1,0:T(8,128)}) fusion(f32[512,1024]{1,0:T(8,128)S(1)} %bitcast_select_fusion, f32[512]{0:T(512)S(1)} %select_bitcast_fusion), kind=kLoop, calls=%fused_computation.23 | loop fusion | flops 261888 | bytes 4197376 | tf_op jit(solution)/shard_map/slice | solution.py:388
  7.1 0.0 copy-start.1
  7.1 0.0 copy-start.2
  7.1 0.6 broadcast_in_dim.20.v_ref
  7.8 23.0 %gather.18 = (f32[1024,1024]{1,0:T(8,128)}, f32[8,8,256]{2,1,0:T(8,128)}) custom-call(f32[256,512]{1,0:T(8,128)} %get-tuple-element.38.piece_ref, f32[8,256]{1,0:T(8,128)} %broadcast_in_dim.20.v_ref), custom_call_target="tpu_custom_call" | custom-call | tf_op jit(solution)/shard_map/gather/pallas_call | solution.py:399
  30.8 0.0 copy-start.7
  30.8 0.0 copy-start.8
  30.8 0.5 collective-permute-start.2
  31.3 0.7 collective-permute-start.1
  32.1 1.0 collective-permute-start
  33.1 0.0 collective-permute-start.3
  33.1 40.9 %factor.1 = (f32[1024,1024]{1,0:T(8,128)}, f32[1024,128]{1,0:T(8,128)}) custom-call(f32[1024,1024]{1,0:T(8,128)} %get-tuple-element.16.a_ref), custom_call_target="tpu_custom_call" | custom-call | flops 64424509440 | bytes 8388608 | tf_op jit(solution)/shard_map/factor/pallas_call | solution.py:427
  74.1 0.0 copy-done.1
  74.1 0.0 copy-done.2
  74.1 0.0 copy-done.7
  74.1 0.6 copy.10
  74.7 0.0 collective-permute-done.3.refs_3_
  74.7 0.0 copy-start.6
  74.7 0.0 collective-permute-done.2.refs_2_
  74.7 0.0 copy-start.3
  74.7 0.0 collective-permute-done.1.refs_1_
  74.7 0.0 copy-start.4
  74.7 0.0 collective-permute-done.refs_0_
  74.7 0.0 copy-start.5
  74.8 0.0 copy-done.8
  74.8 0.7 broadcast_in_dim.35.noise_ref
  75.5 0.0 copy-done.6
  75.5 0.2 copy-done.3
  75.7 0.2 copy-done.4
  75.9 0.1 copy-done.5
  76.0 11.4 %forward.1 = (f32[256,512]{1,0:T(8,128)}, f32[8,1024]{1,0:T(8,128)}) custom-call(f32[1024,1024]{1,0:T(8,128)} %get-tuple-element.17.u_ref, f32[1024,128]{1,0:T(8,128)} %get-tuple-element.18.inv_ref, f32[256,512]{1,0:T(8,128)} %copy-done.2, f32[256,512]{1,0:T(8,128)} %get-tuple-element.34.tile_ref, f32[8,1024]{1,0:T(8,128)} %bitcast.41, ...), custom_call_target="tpu_custom_call" | custom-call | tf_op jit(solution)/shard_map/forward/pallas_call | solution.py:442
  87.5 16.2 %exchange.1 = (f32[4,2,32,512]{3,2,1,0:T(8,128)}, f32[8,1024]{1,0:T(8,128)}) custom-call(f32[256,512]{1,0:T(8,128)} %get-tuple-element.22.s_ref, f32[1024,1024]{1,0:T(8,128)} %get-tuple-element.17.u_ref, f32[1024,128]{1,0:T(8,128)} %get-tuple-element.18.inv_ref, f32[8,1024]{1,0:T(8,128)} %get-tuple-element.23.b_ref), custom_call_target="tpu_custom_call" | custom-call | tf_op jit(solution)/shard_map/exchange/pallas_call | solution.py:461
  103.7 9.6 %place.1 = (f32[12,768,128]{2,1,0:T(8,128)}, f32[1,1024]{1,0:T(1,128)}) custom-call(s32[4,8]{1,0:T(4,128)} %map_ref.1, f32[12,768,128]{2,1,0:T(8,128)} %bitcast.39, f32[4,2,32,512]{3,2,1,0:T(8,128)} %get-tuple-element.24.arrived_ref, f32[8,1024]{1,0:T(8,128)} %get-tuple-element.25.sample_ref), custom_call_target="tpu_custom_call" | custom-call | tf_op jit(solution)/shard_map/place/pallas_call | solution.py:481
  (8 shorter events, 0.1 us)
Async XLA Ops:
  0.6 2.4 %copy-start = (f32[6144]{0:T(1024)S(1)}, f32[6144]{0:T(1024)}, u32[]{:S(2)}) copy-start(f32[6144]{0:T(1024)} %param.11) | copy-start | bytes 73732
  7.1 66.9 %copy-start.1 = (f32[256,512]{1,0:T(8,128)}, f32[256,512]{1,0:T(8,128)S(1)}, u32[]{:S(2)}) copy-start(f32[256,512]{1,0:T(8,128)S(1)} %get-tuple-element.21.refs_4_) | copy-start | bytes 1572868
  7.1 66.9 %copy-start.2 = (f32[256,512]{1,0:T(8,128)}, f32[256,512]{1,0:T(8,128)S(1)}, u32[]{:S(2)}) copy-start(f32[256,512]{1,0:T(8,128)S(1)} %get-tuple-element.20.near_ref) | copy-start | bytes 1572868
  30.8 43.3 %copy-start.7 = (f32[8,8,256]{2,1,0:T(8,128)S(1)}, f32[8,8,256]{2,1,0:T(8,128)}, u32[]{:S(2)}) copy-start(f32[8,8,256]{2,1,0:T(8,128)} %get-tuple-element.19) | copy-start | bytes 196612
  30.8 44.0 %copy-start.8 = (f32[1,1024]{1,0:T(1,128)S(1)}, f32[1,1024]{1,0:T(1,128)}, u32[]{:S(2)}) copy-start(f32[1,1024]{1,0:T(1,128)} %param.10) | copy-start | bytes 12292
  30.8 43.9 %collective-permute-start.2 = (f32[256,512]{1,0:T(8,128)S(1)}, f32[256,512]{1,0:T(8,128)S(1)}, u32[]{:S(2)}, u32[]{:S(2)}) collective-permute-start(f32[256,512]{1,0:T(8,128)S(1)} %get-tuple-element.20.near_ref), channel_id=1, source_target_pairs={{3,0},{0,1},{1,2},{2,3},{7,4},{4,5},{5,6},{6,7},{11,8},{8,9},{9,10... | collective-permute-start | bytes 1572872 | tf_op jit(solution)/shard_map/ppermute | solution.py:422
  31.3 43.4 %collective-permute-start.1 = (f32[256,512]{1,0:T(8,128)S(1)}, f32[256,512]{1,0:T(8,128)S(1)}, u32[]{:S(2)}, u32[]{:S(2)}) collective-permute-start(f32[256,512]{1,0:T(8,128)S(1)} %get-tuple-element.20.near_ref), channel_id=1, source_target_pairs={{2,0},{3,1},{0,2},{1,3},{6,4},{7,5},{4,6},{5,7},{10,8},{11,9},{8,1... | collective-permute-start | bytes 1572872 | tf_op jit(solution)/shard_map/ppermute | solution.py:422
  32.1 42.7 %collective-permute-start = (f32[256,512]{1,0:T(8,128)S(1)}, f32[256,512]{1,0:T(8,128)S(1)}, u32[]{:S(2)}, u32[]{:S(2)}) collective-permute-start(f32[256,512]{1,0:T(8,128)S(1)} %get-tuple-element.20.near_ref), channel_id=1, source_target_pairs={{1,0},{2,1},{3,2},{0,3},{5,4},{6,5},{7,6},{4,7},{9,8},{10,9},{11,1... | collective-permute-start | bytes 1572872 | tf_op jit(solution)/shard_map/ppermute | solution.py:422
  33.1 41.6 %collective-permute-start.3 = (f32[256,512]{1,0:T(8,128)S(1)}, f32[256,512]{1,0:T(8,128)S(1)}, u32[]{:S(2)}, u32[]{:S(2)}) collective-permute-start(f32[256,512]{1,0:T(8,128)S(1)} %get-tuple-element.21.refs_4_), channel_id=1, source_target_pairs={{4,0},{0,4},{5,1},{1,5},{6,2},{2,6},{7,3},{3,7},{12,8},{8,12},{13,... | collective-permute-start | bytes 1572872 | tf_op jit(solution)/shard_map/ppermute | solution.py:422
  74.7 0.8 copy-start.6
  74.7 1.0 copy-start.3
  74.7 1.2 %copy-start.4 = (f32[256,512]{1,0:T(8,128)}, f32[256,512]{1,0:T(8,128)S(1)}, u32[]{:S(2)}) copy-start(f32[256,512]{1,0:T(8,128)S(1)} %collective-permute-done.1.refs_1_) | copy-start | bytes 1572868
  74.7 1.3 %copy-start.5 = (f32[256,512]{1,0:T(8,128)}, f32[256,512]{1,0:T(8,128)S(1)}, u32[]{:S(2)}) copy-start(f32[256,512]{1,0:T(8,128)S(1)} %collective-permute-done.refs_0_) | copy-start | bytes 1572868

commit v3 on v1

--- a/solution.py
+++ b/solution.py
@@ -333,12 +333,15 @@
         copy.wait()
 
 
-def place_kernel(col_count, row_count, share, map_ref, top_ref, arrived_ref, out_ref):
+def place_kernel(
+    col_count, row_count, share, map_ref, top_ref, arrived_ref, sample_ref, out_ref, x_ref
+):
     groups, n_a = arrived_ref.shape[0], arrived_ref.shape[1]
     lanes = top_ref.shape[2]
     rows = top_ref.shape[1] // share
     my_row, my_col = lax.axis_index("row"), lax.axis_index("col")
     out_ref[...] = top_ref[...]
+    x_ref[...] = sample_ref[:1, :]
     for g in range(groups):
         for a in range(n_a):
             ct = map_ref[g, a * col_count + my_col] // col_count
@@ -473,14 +476,17 @@
         name="exchange",
     )(schur, upper, inverse, rhs)
     top = top_front.reshape(top_cols, share * top_rows, block)
-    top_out = pl.pallas_call(
+    top_out, sample = pl.pallas_call(
         functools.partial(place_kernel, col_count, row_count, share),
-        out_shape=jax.ShapeDtypeStruct(top.shape, jnp.float32),
-        in_specs=[SMEM, VMEM, VMEM],
-        out_specs=VMEM,
+        out_shape=(
+            jax.ShapeDtypeStruct(top.shape, jnp.float32),
+            jax.ShapeDtypeStruct((1, pivot_total), jnp.float32),
+        ),
+        in_specs=[SMEM, VMEM, VMEM, VMEM],
+        out_specs=(VMEM, VMEM),
         name="place",
-    )(block_map, top, arrived)
-    return (top_out.reshape(top_front.shape), solved[:1])
+    )(block_map, top, arrived, solved)
+    return (top_out.reshape(top_front.shape), sample)
 
 
 def solution(mesh):

time: 112 us -> 110 us (0.982)
  local copies, waits for them, and re-layouts: 5.83 us -> 4.44 us
    slice x1 -> x0, local copies, waits for them, and re-layouts: 1.35 us -> none  [local(): return (top_out.reshape(top_front.shape), solved[:1])]
where the time goes in v3:
time: 110 us; the launch traced here: 109 us
  Pallas kernels  97.2 us (88%)
  local copies, waits for them, and re-layouts  4.44 us (4%)
  other arithmetic  3.9 us (4%)
  starting transfers between devices  2.31 us (2%)
  between operations  1.45 us (1%)
    pallas_call x1, Pallas kernels, local(): pl.pallas_call(factor_kernel, out_shape=(jax.ShapeDtypeStruct((pivot_tota...  40.9 us
    pallas_call x1, Pallas kernels, local(): pl.pallas_call(functools.partial(gather_kernel, row_count, col_count, blo...  23 us
    pallas_call x1, Pallas kernels, local(): pl.pallas_call(functools.partial(exchange_kernel, share), out_shape=(jax....  16.2 us
    pallas_call x1, Pallas kernels, local(): pl.pallas_call(functools.partial(solve_kernel, col_count, row_count), out...  11.7 us
    pallas_call x1, Pallas kernels, local(): pl.pallas_call(functools.partial(place_kernel, col_count, row_count, shar...  5.32 us
    select_n x1, other arithmetic, local(): tile = jnp.where(keep, tile, unit)  2.33 us
    ppermute x4, starting transfers between devices, shifted(): return lax.ppermute(value, axis, pairs)  2.31 us
  transfers between devices with their start and end apart: 4, of which 0 were waited for; matrix products, arithmetic and copies ran while one was open for 1% of the time, Pallas kernels for 37%

profile of v3, /device:TPU:0, one launch (start us, length us, event | category | flops | bytes accessed | tf_op | source)
XLA Modules:
  0.0 109.3 jit_solution(3553329147284775349)
XLA Ops:
  0.6 0.0 copy-start
  0.7 0.7 dynamic-slice_bitcast_fusion
  1.4 0.6 gather_fusion
  2.7 0.1 add_bitcast_fusion.1
  2.8 0.1 and_not_fusion.1
  2.9 0.1 add_bitcast_fusion
  2.9 0.1 and_not_fusion
  3.0 0.0 copy-done
  3.0 0.6 gather_fusion.1
  3.6 0.1 select_bitcast_fusion
  3.7 2.3 %bitcast_select_fusion = f32[512,1024]{1,0:T(8,128)S(1)} fusion(f32[64,8,8,128]{3,2,1,0:T(8,128)} %bitcast.40, s32[1024]{0:T(1024)S(1)} %add_bitcast_fusion, s32[512]{0:T(512)S(1)} %add_bitcast_fusion.1, pred[1024]{0:T(1024)(128)(4,1)S(1)} %and_not_fusion, pred[512]{0:T(512)(128)(4,1)S(1)} %and_not_fusion.1), kind=kLoop, calls=%fused_computation.2 | loop fusion | flops 2097152 | bytes 4201984 | tf_op jit(solution)/shard_map/jit(_where)/select_n | solution.py:378
  6.0 1.1 %fusion.2 = (f32[256,512]{1,0:T(8,128)}, f32[256]{0:T(256)S(1)}, f32[256,512]{1,0:T(8,128)S(1)}, f32[256,512]{1,0:T(8,128)S(1)}, f32[256,512]{1,0:T(8,128)}) fusion(f32[512,1024]{1,0:T(8,128)S(1)} %bitcast_select_fusion, f32[512]{0:T(512)S(1)} %select_bitcast_fusion), kind=kLoop, calls=%fused_computation.23 | loop fusion | flops 261888 | bytes 4197376 | tf_op jit(solution)/shard_map/slice | solution.py:387
  7.1 0.0 copy-start.1
  7.1 0.0 copy-start.2
  7.1 0.6 broadcast_in_dim.20.v_ref
  7.8 23.0 %gather.18 = (f32[1024,1024]{1,0:T(8,128)}, f32[8,8,256]{2,1,0:T(8,128)}) custom-call(f32[256,512]{1,0:T(8,128)} %get-tuple-element.38.piece_ref, f32[8,256]{1,0:T(8,128)} %broadcast_in_dim.20.v_ref), custom_call_target="tpu_custom_call" | custom-call | tf_op jit(solution)/shard_map/gather/pallas_call | solution.py:398
  30.8 0.0 copy-start.7
  30.8 0.0 copy-start.8
  30.8 0.5 collective-permute-start.2
  31.3 0.7 collective-permute-start.1
  32.1 1.0 collective-permute-start
  33.1 0.0 collective-permute-start.3
  33.1 40.9 %factor.1 = (f32[1024,1024]{1,0:T(8,128)}, f32[1024,128]{1,0:T(8,128)}) custom-call(f32[1024,1024]{1,0:T(8,128)} %get-tuple-element.16.a_ref), custom_call_target="tpu_custom_call" | custom-call | flops 64424509440 | bytes 8388608 | tf_op jit(solution)/shard_map/factor/pallas_call | solution.py:426
  74.1 0.0 copy-done.1
  74.1 0.0 copy-done.2
  74.1 0.0 copy-done.7
  74.1 0.6 copy.10
  74.7 0.0 collective-permute-done.3.refs_3_
  74.7 0.0 copy-start.6
  74.7 0.0 collective-permute-done.2.refs_2_
  74.7 0.0 copy-start.3
  74.7 0.0 collective-permute-done.1.refs_1_
  74.7 0.0 copy-start.4
  74.7 0.0 collective-permute-done.refs_0_
  74.7 0.0 copy-start.5
  74.8 0.0 copy-done.8
  74.8 0.7 broadcast_in_dim.35.noise_ref
  75.5 0.0 copy-done.6
  75.5 0.2 copy-done.3
  75.7 0.2 copy-done.4
  75.9 0.1 copy-done.5
  76.0 11.7 %forward.1 = (f32[256,512]{1,0:T(8,128)}, f32[8,1024]{1,0:T(8,128)}) custom-call(f32[1024,1024]{1,0:T(8,128)} %get-tuple-element.17.u_ref, f32[1024,128]{1,0:T(8,128)} %get-tuple-element.18.inv_ref, f32[256,512]{1,0:T(8,128)} %copy-done.2, f32[256,512]{1,0:T(8,128)} %get-tuple-element.34.tile_ref, f32[8,1024]{1,0:T(8,128)} %bitcast.41, ...), custom_call_target="tpu_custom_call" | custom-call | tf_op jit(solution)/shard_map/forward/pallas_call | solution.py:441
  87.7 16.2 %exchange.1 = (f32[4,2,32,512]{3,2,1,0:T(8,128)}, f32[8,1024]{1,0:T(8,128)}) custom-call(f32[256,512]{1,0:T(8,128)} %get-tuple-element.22.s_ref, f32[1024,1024]{1,0:T(8,128)} %get-tuple-element.17.u_ref, f32[1024,128]{1,0:T(8,128)} %get-tuple-element.18.inv_ref, f32[8,1024]{1,0:T(8,128)} %get-tuple-element.23.b_ref), custom_call_target="tpu_custom_call" | custom-call | tf_op jit(solution)/shard_map/exchange/pallas_call | solution.py:460
  103.9 5.3 %place.1 = (f32[12,768,128]{2,1,0:T(8,128)}, f32[1,1024]{1,0:T(1,128)}) custom-call(s32[4,8]{1,0:T(4,128)} %map_ref.1, f32[12,768,128]{2,1,0:T(8,128)} %bitcast.39, f32[4,2,32,512]{3,2,1,0:T(8,128)} %get-tuple-element.24.arrived_ref, f32[8,1024]{1,0:T(8,128)} %get-tuple-element.25.sample_ref), custom_call_target="tpu_custom_call" | custom-call | tf_op jit(solution)/shard_map/place/pallas_call | solution.py:479
  (8 shorter events, 0.1 us)
Async XLA Ops:
  0.6 2.4 %copy-start = (f32[6144]{0:T(1024)S(1)}, f32[6144]{0:T(1024)}, u32[]{:S(2)}) copy-start(f32[6144]{0:T(1024)} %param.11) | copy-start | bytes 73732
  7.1 66.9 %copy-start.1 = (f32[256,512]{1,0:T(8,128)}, f32[256,512]{1,0:T(8,128)S(1)}, u32[]{:S(2)}) copy-start(f32[256,512]{1,0:T(8,128)S(1)} %get-tuple-element.21.refs_4_) | copy-start | bytes 1572868
  7.1 66.9 %copy-start.2 = (f32[256,512]{1,0:T(8,128)}, f32[256,512]{1,0:T(8,128)S(1)}, u32[]{:S(2)}) copy-start(f32[256,512]{1,0:T(8,128)S(1)} %get-tuple-element.20.near_ref) | copy-start | bytes 1572868
  30.8 43.3 %copy-start.7 = (f32[8,8,256]{2,1,0:T(8,128)S(1)}, f32[8,8,256]{2,1,0:T(8,128)}, u32[]{:S(2)}) copy-start(f32[8,8,256]{2,1,0:T(8,128)} %get-tuple-element.19) | copy-start | bytes 196612
  30.8 44.0 %copy-start.8 = (f32[1,1024]{1,0:T(1,128)S(1)}, f32[1,1024]{1,0:T(1,128)}, u32[]{:S(2)}) copy-start(f32[1,1024]{1,0:T(1,128)} %param.10) | copy-start | bytes 12292
  30.8 43.9 %collective-permute-start.2 = (f32[256,512]{1,0:T(8,128)S(1)}, f32[256,512]{1,0:T(8,128)S(1)}, u32[]{:S(2)}, u32[]{:S(2)}) collective-permute-start(f32[256,512]{1,0:T(8,128)S(1)} %get-tuple-element.20.near_ref), channel_id=1, source_target_pairs={{3,0},{0,1},{1,2},{2,3},{7,4},{4,5},{5,6},{6,7},{11,8},{8,9},{9,10... | collective-permute-start | bytes 1572872 | tf_op jit(solution)/shard_map/ppermute | solution.py:421
  31.3 43.4 %collective-permute-start.1 = (f32[256,512]{1,0:T(8,128)S(1)}, f32[256,512]{1,0:T(8,128)S(1)}, u32[]{:S(2)}, u32[]{:S(2)}) collective-permute-start(f32[256,512]{1,0:T(8,128)S(1)} %get-tuple-element.20.near_ref), channel_id=1, source_target_pairs={{2,0},{3,1},{0,2},{1,3},{6,4},{7,5},{4,6},{5,7},{10,8},{11,9},{8,1... | collective-permute-start | bytes 1572872 | tf_op jit(solution)/shard_map/ppermute | solution.py:421
  32.1 42.7 %collective-permute-start = (f32[256,512]{1,0:T(8,128)S(1)}, f32[256,512]{1,0:T(8,128)S(1)}, u32[]{:S(2)}, u32[]{:S(2)}) collective-permute-start(f32[256,512]{1,0:T(8,128)S(1)} %get-tuple-element.20.near_ref), channel_id=1, source_target_pairs={{1,0},{2,1},{3,2},{0,3},{5,4},{6,5},{7,6},{4,7},{9,8},{10,9},{11,1... | collective-permute-start | bytes 1572872 | tf_op jit(solution)/shard_map/ppermute | solution.py:421
  33.1 41.6 %collective-permute-start.3 = (f32[256,512]{1,0:T(8,128)S(1)}, f32[256,512]{1,0:T(8,128)S(1)}, u32[]{:S(2)}, u32[]{:S(2)}) collective-permute-start(f32[256,512]{1,0:T(8,128)S(1)} %get-tuple-element.21.refs_4_), channel_id=1, source_target_pairs={{4,0},{0,4},{5,1},{1,5},{6,2},{2,6},{7,3},{3,7},{12,8},{8,12},{13,... | collective-permute-start | bytes 1572872 | tf_op jit(solution)/shard_map/ppermute | solution.py:421
  74.7 0.8 copy-start.6
  74.7 1.0 copy-start.3
  74.7 1.2 %copy-start.4 = (f32[256,512]{1,0:T(8,128)}, f32[256,512]{1,0:T(8,128)S(1)}, u32[]{:S(2)}) copy-start(f32[256,512]{1,0:T(8,128)S(1)} %collective-permute-done.1.refs_1_) | copy-start | bytes 1572868
  74.7 1.3 %copy-start.5 = (f32[256,512]{1,0:T(8,128)}, f32[256,512]{1,0:T(8,128)S(1)}, u32[]{:S(2)}) copy-start(f32[256,512]{1,0:T(8,128)S(1)} %collective-permute-done.refs_0_) | copy-start | bytes 1572868
